TPU v7x, 512 devices: a whole 4x4x16 slice. The times are simulated.
512 devices in a mesh: region: 64 (over z, x), split: 8 (over y, core).
Axes of the slice: x: 4, y: 4, z: 16, core: 2. Of those that a mesh axis runs over, the one named last changes fastest.
Arguments:
- vectors: float32 [294912, 256], P(('region', 'split'))
- hessian: bfloat16 [1536, 12, 192, 192], P(('region', 'split')), may hold values from -0.125 to 0.125
- block_cols: int32 [1536, 12], P(('region', 'split')), may hold values from 0 to 35, as said below
- live_blocks: int32 [1536], P(('region', 'split')), may hold values from 6 to 12, as said below
- halo_lists: int32 [64, 2, 6], P('region'), may hold values from 0 to 23, as said below
- bounds: float32 [2], replicated, as said below
Outputs:
- basis: float32 [294912, 256], P(('region', 'split'))
- projected: float32 [256, 256], replicated
Inputs may be any that keep to these rules, and one draw needn't show every extreme that they name: `block_cols`: in each row the entries are distinct and entry 0 is the row's own block within its region; values below 24 name blocks of the row's region, 24 + j the j-th block received from the lower region, 30 + j the j-th from the upper region. `live_blocks`: the first block row of every region has all 12 blocks intact. `halo_lists`: each list holds distinct block indices within the region. bounds[0] < 0 < bounds[1].
All inputs are finite; a program needn't handle non-finite values.
Results may differ from a plain program's by a relative error of at most 0.0005.
The roundings to bfloat16 on the way count: a program that leaves them out, or rounds other values in their place, can miss the bound.
Values may be sent and summed in bfloat16 or wider, within the bound.
A program may use at most 64 MiB of HBM per device.

v0:
```python
import jax
import jax.numpy as jnp
from jax import lax
from jax.sharding import PartitionSpec as P


def shifted(value, axis, steps):
    count = lax.axis_size(axis)
    pairs = [(source, (source + steps) % count) for source in range(count)]
    return lax.ppermute(value, axis, pairs)


def apply_blocks(operand, hessian, block_cols, live_blocks, halo_lists):
    row_blocks = hessian.shape[0]
    block_size = hessian.shape[2]
    mode_count = operand.shape[1]
    shard_blocks = operand.reshape(row_blocks, block_size, mode_count)
    region = lax.all_gather(shard_blocks, "split", axis=0, tiled=True)
    send_lower = region[halo_lists[0, 0]]
    send_upper = region[halo_lists[0, 1]]
    from_lower = shifted(send_upper, "region", 1)
    from_upper = shifted(send_lower, "region", -1)
    candidates = jnp.concatenate([region, from_lower, from_upper], 0)
    picked = candidates[block_cols]
    used_mask = lax.broadcasted_iota(jnp.int32, block_cols.shape, 1) < live_blocks[:, None]
    picked = jnp.where(used_mask[:, :, None, None], picked, jnp.zeros((), jnp.bfloat16))
    product = jnp.einsum("rkij,rkjm->rim", hessian, picked, preferred_element_type=jnp.float32)
    return product.reshape(row_blocks * block_size, mode_count)


def local(vectors, hessian, block_cols, live_blocks, halo_lists, bounds):
    centre = 0.5 * (bounds[0] + bounds[1])
    half_width = 0.5 * (bounds[1] - bounds[0])
    first = apply_blocks(vectors.astype(jnp.bfloat16), hessian, block_cols, live_blocks, halo_lists)
    filtered_one = (first - centre * vectors) / half_width
    second = apply_blocks(
        filtered_one.astype(jnp.bfloat16), hessian, block_cols, live_blocks, halo_lists
    )
    filtered_two = 2.0 * (second - centre * filtered_one) / half_width - vectors
    image = apply_blocks(
        filtered_two.astype(jnp.bfloat16), hessian, block_cols, live_blocks, halo_lists
    )
    total_rows = vectors.shape[0] * lax.axis_size("region") * lax.axis_size("split")
    contract = (((0,), (0,)), ((), ()))
    gram_part = lax.dot_general(
        filtered_two, filtered_two, contract, precision=lax.Precision.HIGHEST
    )
    cross_part = lax.dot_general(filtered_two, image, contract, precision=lax.Precision.HIGHEST)
    gram, cross = lax.psum((gram_part, cross_part), ("region", "split"))
    gram = gram / total_rows
    cross = cross / total_rows
    lower = jnp.linalg.cholesky(gram)
    basis = jax.scipy.linalg.solve_triangular(lower, filtered_two.T, lower=True).T
    partial_left = jax.scipy.linalg.solve_triangular(lower, cross, lower=True)
    projected = jax.scipy.linalg.solve_triangular(lower, partial_left.T, lower=True).T
    return (basis, projected)


def solution(mesh):
    placed = (
        P(("region", "split"), None),
        P(("region", "split"), None, None, None),
        P(("region", "split"), None),
        P(("region", "split")),
        P("region", None, None),
        P(),
    )
    return jax.shard_map(
        local,
        mesh=mesh,
        in_specs=placed,
        out_specs=(P(("region", "split"), None), P()),
        check_vma=False,
    )
```

profile of v0, /device:TPU:1, one launch (start us, length us, event | category | flops | bytes accessed | tf_op | source)
XLA Modules:
  0.0 814.2 jit_solution(8782221556383976657)
XLA Ops:
  10.1 39.6 %all-gather.4.cloned.1.call-done = bf16[24,192,256]{2,1,0:T(8,128)(2,1)} async-done(((bf16[3,192,256]{2,1,0:T(8,128)(2,1)}), bf16[24,192,256]{2,1,0:T(8,128)(2,1)}) %all-gather.4.cloned.1.call-update) | async-done | bytes 2359312 | tf_op jit(solution)/shard_map/all_gather | solution.py:18
  59.0 6.6 collective-permute-start.1
  69.7 4.6 collective-permute-done
  74.3 4.0 collective-permute-done.1
  78.3 3.4 pad_maximum_fusion
  81.7 4.8 gather_fusion.2
  90.6 34.4 %all-gather.6.cloned.1.call-done = bf16[24,192,256]{2,1,0:T(8,128)(2,1)} async-done(((bf16[3,192,256]{2,1,0:T(8,128)(2,1)}), bf16[24,192,256]{2,1,0:T(8,128)(2,1)}) %all-gather.6.cloned.1.call-update) | async-done | bytes 2359312 | tf_op jit(solution)/shard_map/all_gather | solution.py:18
  134.3 6.6 collective-permute-start.3
  141.0 8.7 %collective-permute-done.2 = bf16[6,192,256]{2,1,0:T(8,128)(2,1)} collective-permute-done((bf16[6,192,256]{2,1,0:T(8,128)(2,1)}, bf16[6,192,256]{2,1,0:T(8,128)(2,1)}, u32[]{:S(2)}, u32[]{:S(2)}) %collective-permute-start.2) | collective-permute-done | bytes 589856 | tf_op jit(solution)/shard_map/ppermute | solution.py:10
  149.7 4.0 collective-permute-done.3
  153.7 3.3 pad_maximum_fusion.1
  157.0 4.8 gather_fusion.5
  166.1 34.3 %all-gather.8.cloned.1.call-done = bf16[24,192,256]{2,1,0:T(8,128)(2,1)} async-done(((bf16[3,192,256]{2,1,0:T(8,128)(2,1)}), bf16[24,192,256]{2,1,0:T(8,128)(2,1)}) %all-gather.8.cloned.1.call-update) | async-done | bytes 2359312 | tf_op jit(solution)/shard_map/all_gather | solution.py:18
  209.8 6.6 collective-permute-start.5
  219.6 5.5 collective-permute-done.4
  225.1 4.0 collective-permute-done.5
  229.1 3.3 pad_maximum_fusion.2
  232.5 4.8 gather_fusion.8
  242.3 466.4 %all-reduce.4.cloned.1.call-done = (f32[256,256]{0,1:T(8,128)}, f32[256,256]{0,1:T(8,128)}) async-done(((f32[256,256]{0,1:T(8,128)}, f32[256,256]{0,1:T(8,128)}), (f32[256,256]{0,1:T(8,128)}, f32[256,256]{0,1:T(8,128)})) %all-reduce.4.cloned.1.call-update) | async-done | bytes 524304 | tf_op jit(solution)/shard_map/psum | solution.py:49
  714.8 13.2 %cholesky.50 = f32[128,128]{1,0:T(8,128)} custom-call(f32[128,128]{1,0:T(8,128)} %cholesky.118), custom_call_target="Cholesky" | custom-call | tf_op jit(solution)/shard_map/jit(cholesky)/cholesky | solution.py:52
  731.0 11.3 %custom-call.18 = f32[1,128,128]{1,2,0:T(8,128)} custom-call(f32[1,128,128]{2,1,0:T(8,128)} %get-tuple-element.48), custom_call_target="InvertDiagBlocksLowerTriangular" | custom-call | tf_op jit(solution)/shard_map/jit(cholesky)/cholesky | solution.py:52
  745.7 13.4 %cholesky.105 = f32[128,128]{1,0:T(8,128)} custom-call(f32[128,128]{1,0:T(8,128)} %convolution_subtract_fusion.3), custom_call_target="Cholesky" | custom-call | tf_op jit(solution)/shard_map/jit(cholesky)/cholesky | solution.py:52
  765.0 6.9 while.5
  771.8 21.1 %custom-call.19 = f32[2,128,128]{1,2,0:T(8,128)} custom-call(f32[2,128,128]{2,1,0:T(8,128)} %get-tuple-element.18), custom_call_target="InvertDiagBlocksLowerTriangular" | custom-call | tf_op jit(solution)/shard_map/jit(_solve_triangular)/triangular_solve | solution.py:53
  (85 shorter events, 87.2 us)
Async XLA Ops:
  7.2 79.4 %copy-start = (bf16[3,12,192,192]{3,2,1,0:T(8,128)(2,1)S(1)}, bf16[3,12,192,192]{3,2,1,0:T(8,128)(2,1)}, u32[]{:S(2)}) copy-start(bf16[3,12,192,192]{3,2,1,0:T(8,128)(2,1)} %param.9) | copy-start | bytes 7962628
  7.2 58.4 %copy-start.8 = (f32[2]{0:T(128)S(1)}, f32[2]{0:T(128)}, u32[]{:S(2)}) copy-start(f32[2]{0:T(128)} %param.13) | copy-start | bytes 28
  7.2 61.7 %copy-start.7 = (s32[3,12]{1,0:T(4,128)S(1)}, s32[3,12]{1,0:T(4,128)}, u32[]{:S(2)}) copy-start(s32[3,12]{1,0:T(4,128)} %param.10) | copy-start | bytes 436
  7.2 42.5 %all-gather.4.cloned.1.call-start = ((), (), s32[]{:S(2)}) async-start(), calls=%async_computation | async-start | bytes 2654208 | tf_op jit(solution)/shard_map/all_gather | solution.py:18
  9.2 115.8 %all-gather.6.cloned.1.call-start = ((), (), s32[]{:S(2)}) async-start(), calls=%async_computation.1 | async-start | bytes 2654208 | tf_op jit(solution)/shard_map/all_gather | solution.py:18
  52.8 21.5 %collective-permute-start = (bf16[6,192,256]{2,1,0:T(8,128)(2,1)}, bf16[6,192,256]{2,1,0:T(8,128)(2,1)}, u32[]{:S(2)}, u32[]{:S(2)}) collective-permute-start(bf16[6,192,256]{2,1,0:T(8,128)(2,1)} %gather_fusion), channel_id=1, source_target_pairs={{0,8},{8,16},{16,24},{24,32},{32,40},{40,48},{48,56},{56,64},{64,7... | collective-permute-start | bytes 1769480 | tf_op jit(solution)/shard_map/ppermute | solution.py:10
  59.0 19.3 %collective-permute-start.1 = (bf16[6,192,256]{2,1,0:T(8,128)(2,1)}, bf16[6,192,256]{2,1,0:T(8,128)(2,1)}, u32[]{:S(2)}, u32[]{:S(2)}) collective-permute-start(bf16[6,192,256]{2,1,0:T(8,128)(2,1)} %gather_fusion.1), channel_id=1, source_target_pairs={{0,504},{8,0},{16,8},{24,16},{32,24},{40,32},{48,40},{56,48},{64,5... | collective-permute-start | bytes 1769480 | tf_op jit(solution)/shard_map/ppermute | solution.py:10
  86.6 3.1 copy-start.2
  89.6 0.9 copy-start.4
  90.6 109.9 %all-gather.8.cloned.1.call-start = ((), (), s32[]{:S(2)}) async-start(), calls=%async_computation.2 | async-start | bytes 2654208 | tf_op jit(solution)/shard_map/all_gather | solution.py:18
  128.1 21.5 %collective-permute-start.2 = (bf16[6,192,256]{2,1,0:T(8,128)(2,1)}, bf16[6,192,256]{2,1,0:T(8,128)(2,1)}, u32[]{:S(2)}, u32[]{:S(2)}) collective-permute-start(bf16[6,192,256]{2,1,0:T(8,128)(2,1)} %gather_fusion.3), channel_id=1, source_target_pairs={{0,8},{8,16},{16,24},{24,32},{32,40},{40,48},{48,56},{56,64},{64,7... | collective-permute-start | bytes 1769480 | tf_op jit(solution)/shard_map/ppermute | solution.py:10
  134.3 19.3 %collective-permute-start.3 = (bf16[6,192,256]{2,1,0:T(8,128)(2,1)}, bf16[6,192,256]{2,1,0:T(8,128)(2,1)S(1)}, u32[]{:S(2)}, u32[]{:S(2)}) collective-permute-start(bf16[6,192,256]{2,1,0:T(8,128)(2,1)} %gather_fusion.4), channel_id=1, source_target_pairs={{0,504},{8,0},{16,8},{24,16},{32,24},{40,32},{48,40},{56,48},{64,5... | collective-permute-start | bytes 1769480 | tf_op jit(solution)/shard_map/ppermute | solution.py:10
  161.9 3.1 copy-start.3
  161.9 3.1 copy-start.5
  166.1 542.7 %all-reduce.4.cloned.1.call-start = ((), (), s32[]{:S(2)}) async-start(), calls=%async_computation.3 | async-start | bytes 1048576 | tf_op jit(solution)/shard_map/psum | solution.py:49
  203.6 21.5 %collective-permute-start.4 = (bf16[6,192,256]{2,1,0:T(8,128)(2,1)}, bf16[6,192,256]{2,1,0:T(8,128)(2,1)}, u32[]{:S(2)}, u32[]{:S(2)}) collective-permute-start(bf16[6,192,256]{2,1,0:T(8,128)(2,1)} %gather_fusion.6), channel_id=1, source_target_pairs={{0,8},{8,16},{16,24},{24,32},{32,40},{40,48},{48,56},{56,64},{64,7... | collective-permute-start | bytes 1769480 | tf_op jit(solution)/shard_map/ppermute | solution.py:10
  209.8 19.3 %collective-permute-start.5 = (bf16[6,192,256]{2,1,0:T(8,128)(2,1)}, bf16[6,192,256]{2,1,0:T(8,128)(2,1)S(1)}, u32[]{:S(2)}, u32[]{:S(2)}) collective-permute-start(bf16[6,192,256]{2,1,0:T(8,128)(2,1)} %gather_fusion.7), channel_id=1, source_target_pairs={{0,504},{8,0},{16,8},{24,16},{32,24},{40,32},{48,40},{56,48},{64,5... | collective-permute-start | bytes 1769480 | tf_op jit(solution)/shard_map/ppermute | solution.py:10
  237.3 3.0 copy-start.1
  713.5 0.7 copy-start.6
Sparse Core Ops, SparseCore 0:
  10.7 38.9 all-gather.3
  90.7 34.3 all-gather.5
  166.2 34.2 all-gather.7
  242.4 466.3 all-reduce.3
where the time goes:
time: 816 us; the launch traced here: 814 us
  waiting for transfers between devices  606 us (74%)
  other arithmetic  85.1 us (10%)
  local copies, waits for them, and re-layouts  47.2 us (6%)
  starting transfers between devices  29.3 us (4%)
  matrix products  29 us (4%)
  between operations  18 us (2%)
    psum x1, waiting for transfers between devices, local(): gram, cross = lax.psum((gram_part, cross_part), ('region', 'split'))  466 us
    all_gather x3, waiting for transfers between devices, apply_blocks(): region = lax.all_gather(shard_blocks, 'split', axis=0, tiled=True)  108 us
    another operation x7, other arithmetic, local(): lower = jnp.linalg.cholesky(gram)  42.1 us
    ppermute x6, waiting for transfers between devices, shifted(): return lax.ppermute(value, axis, pairs)  30.8 us
    ppermute x6, starting transfers between devices, shifted(): return lax.ppermute(value, axis, pairs)  29.1 us
    another operation x3, other arithmetic, local(): jax.scipy.linalg.solve_triangular(lower, filtered_two.T, lower=True)  22.8 us
  transfers between devices with their start and end apart: 10, of which 10 were waited for; matrix products, arithmetic and copies ran while one was open for 2% of the time, Pallas kernels for 0%

commit v1 on v0

--- a/solution.py
+++ b/solution.py
@@ -46,7 +46,7 @@
         filtered_two, filtered_two, contract, precision=lax.Precision.HIGHEST
     )
     cross_part = lax.dot_general(filtered_two, image, contract, precision=lax.Precision.HIGHEST)
-    gram, cross = lax.psum((gram_part, cross_part), ("region", "split"))
+    gram, cross = lax.psum(lax.psum((gram_part, cross_part), "split"), "region")
     gram = gram / total_rows
     cross = cross / total_rows
     lower = jnp.linalg.cholesky(gram)

time: 816 us -> 697 us (0.85); the launches traced: 814 us -> 687 us
  waiting for transfers between devices: 606 us -> 478 us
    psum x1 -> x2, waiting for transfers between devices: 466 us -> 339 us  [local(): gram, cross = lax.psum(lax.psum((gram_part, cross_part), 'split'), 'region')]
  transfers between devices with their start and end apart: 10 -> 11, of which waited for: 10 -> 11; matrix products, arithmetic and copies ran while one was open for 2% -> 2% of each run, Pallas kernels for 0% -> 0%
where the time goes in v1:
time: 697 us; the launch traced here: 687 us
  waiting for transfers between devices  478 us (69%)
  other arithmetic  84.8 us (12%)
  local copies, waits for them, and re-layouts  47.1 us (7%)
  starting transfers between devices  29.5 us (4%)
  matrix products  29 us (4%)
  between operations  17.8 us (3%)
    psum x2, waiting for transfers between devices, local(): gram, cross = lax.psum(lax.psum((gram_part, cross_part), 'split'), 'region')  339 us
    all_gather x3, waiting for transfers between devices, apply_blocks(): region = lax.all_gather(shard_blocks, 'split', axis=0, tiled=True)  108 us
    another operation x7, other arithmetic, local(): lower = jnp.linalg.cholesky(gram)  42 us
    ppermute x6, waiting for transfers between devices, shifted(): return lax.ppermute(value, axis, pairs)  31.1 us
    ppermute x6, starting transfers between devices, shifted(): return lax.ppermute(value, axis, pairs)  29.1 us
    another operation x3, other arithmetic, local(): jax.scipy.linalg.solve_triangular(lower, filtered_two.T, lower=True)  22.8 us
    gather x3, local copies, waits for them, and re-layouts, apply_blocks(): picked = candidates[block_cols]  14.5 us
  transfers between devices with their start and end apart: 11, of which 11 were waited for; matrix products, arithmetic and copies ran while one was open for 2% of the time, Pallas kernels for 0%

profile of v1, /device:TPU:1, one launch (start us, length us, event | category | flops | bytes accessed | tf_op | source)
XLA Modules:
  0.0 686.5 jit_solution(2221420616518102281)
XLA Ops:
  10.1 39.6 %all-gather.4.cloned.1.call-done = bf16[24,192,256]{2,1,0:T(8,128)(2,1)} async-done(((bf16[3,192,256]{2,1,0:T(8,128)(2,1)}), bf16[24,192,256]{2,1,0:T(8,128)(2,1)}) %all-gather.4.cloned.1.call-update) | async-done | bytes 2359312 | tf_op jit(solution)/shard_map/all_gather | solution.py:18
  59.0 6.6 collective-permute-start.1
  69.5 4.9 collective-permute-done
  74.3 4.0 collective-permute-done.1
  78.3 3.4 pad_maximum_fusion
  81.7 4.8 gather_fusion.2
  90.6 34.4 %all-gather.6.cloned.1.call-done = bf16[24,192,256]{2,1,0:T(8,128)(2,1)} async-done(((bf16[3,192,256]{2,1,0:T(8,128)(2,1)}), bf16[24,192,256]{2,1,0:T(8,128)(2,1)}) %all-gather.6.cloned.1.call-update) | async-done | bytes 2359312 | tf_op jit(solution)/shard_map/all_gather | solution.py:18
  134.3 6.6 collective-permute-start.3
  140.9 8.7 %collective-permute-done.2 = bf16[6,192,256]{2,1,0:T(8,128)(2,1)} collective-permute-done((bf16[6,192,256]{2,1,0:T(8,128)(2,1)}, bf16[6,192,256]{2,1,0:T(8,128)(2,1)}, u32[]{:S(2)}, u32[]{:S(2)}) %collective-permute-start.2) | collective-permute-done | bytes 589856 | tf_op jit(solution)/shard_map/ppermute | solution.py:10
  149.6 4.0 collective-permute-done.3
  153.6 3.3 pad_maximum_fusion.1
  157.0 4.8 gather_fusion.5
  166.1 34.3 %all-gather.8.cloned.1.call-done = bf16[24,192,256]{2,1,0:T(8,128)(2,1)} async-done(((bf16[3,192,256]{2,1,0:T(8,128)(2,1)}), bf16[24,192,256]{2,1,0:T(8,128)(2,1)}) %all-gather.8.cloned.1.call-update) | async-done | bytes 2359312 | tf_op jit(solution)/shard_map/all_gather | solution.py:18
  209.7 6.6 collective-permute-start.5
  219.5 5.5 collective-permute-done.4
  225.0 4.0 collective-permute-done.5
  232.3 4.8 gather_fusion.8
  242.4 75.6 %all-reduce.8.cloned.1.call-done = (f32[256,256]{0,1:T(8,128)}, f32[256,256]{0,1:T(8,128)}) async-done(((f32[256,256]{0,1:T(8,128)}, f32[256,256]{0,1:T(8,128)}), (f32[256,256]{0,1:T(8,128)}, f32[256,256]{0,1:T(8,128)})) %all-reduce.8.cloned.1.call-update) | async-done | bytes 524304 | tf_op jit(solution)/shard_map/psum | solution.py:49
  318.1 263.2 %all-reduce.6.cloned.1.call-done = (f32[256,256]{0,1:T(8,128)}, f32[256,256]{0,1:T(8,128)}) async-done(((f32[256,256]{0,1:T(8,128)}, f32[256,256]{0,1:T(8,128)}), (f32[256,256]{0,1:T(8,128)}, f32[256,256]{0,1:T(8,128)})) %all-reduce.6.cloned.1.call-update) | async-done | bytes 524304 | tf_op jit(solution)/shard_map/psum | solution.py:49
  587.3 13.2 %cholesky.50 = f32[128,128]{1,0:T(8,128)} custom-call(f32[128,128]{1,0:T(8,128)} %cholesky.118), custom_call_target="Cholesky" | custom-call | tf_op jit(solution)/shard_map/jit(cholesky)/cholesky | solution.py:52
  603.5 11.3 %custom-call.18 = f32[1,128,128]{1,2,0:T(8,128)} custom-call(f32[1,128,128]{2,1,0:T(8,128)} %get-tuple-element.50), custom_call_target="InvertDiagBlocksLowerTriangular" | custom-call | tf_op jit(solution)/shard_map/jit(cholesky)/cholesky | solution.py:52
  618.3 13.2 %cholesky.105 = f32[128,128]{1,0:T(8,128)} custom-call(f32[128,128]{1,0:T(8,128)} %convolution_subtract_fusion.3), custom_call_target="Cholesky" | custom-call | tf_op jit(solution)/shard_map/jit(cholesky)/cholesky | solution.py:52
  637.3 6.8 while.5
  644.2 21.1 %custom-call.19 = f32[2,128,128]{1,2,0:T(8,128)} custom-call(f32[2,128,128]{2,1,0:T(8,128)} %get-tuple-element.18), custom_call_target="InvertDiagBlocksLowerTriangular" | custom-call | tf_op jit(solution)/shard_map/jit(_solve_triangular)/triangular_solve | solution.py:53
  (88 shorter events, 90.7 us)
Async XLA Ops:
  7.2 79.4 %copy-start = (bf16[3,12,192,192]{3,2,1,0:T(8,128)(2,1)S(1)}, bf16[3,12,192,192]{3,2,1,0:T(8,128)(2,1)}, u32[]{:S(2)}) copy-start(bf16[3,12,192,192]{3,2,1,0:T(8,128)(2,1)} %param.9) | copy-start | bytes 7962628
  7.2 58.4 %copy-start.8 = (f32[2]{0:T(128)S(1)}, f32[2]{0:T(128)}, u32[]{:S(2)}) copy-start(f32[2]{0:T(128)} %param.13) | copy-start | bytes 28
  7.2 61.4 %copy-start.7 = (s32[3,12]{1,0:T(4,128)S(1)}, s32[3,12]{1,0:T(4,128)}, u32[]{:S(2)}) copy-start(s32[3,12]{1,0:T(4,128)} %param.10) | copy-start | bytes 436
  7.2 42.5 %all-gather.4.cloned.1.call-start = ((), (), s32[]{:S(2)}) async-start(), calls=%async_computation | async-start | bytes 2654208 | tf_op jit(solution)/shard_map/all_gather | solution.py:18
  9.2 115.8 %all-gather.6.cloned.1.call-start = ((), (), s32[]{:S(2)}) async-start(), calls=%async_computation.1 | async-start | bytes 2654208 | tf_op jit(solution)/shard_map/all_gather | solution.py:18
  52.8 21.5 %collective-permute-start = (bf16[6,192,256]{2,1,0:T(8,128)(2,1)}, bf16[6,192,256]{2,1,0:T(8,128)(2,1)}, u32[]{:S(2)}, u32[]{:S(2)}) collective-permute-start(bf16[6,192,256]{2,1,0:T(8,128)(2,1)} %gather_fusion), channel_id=1, source_target_pairs={{0,8},{8,16},{16,24},{24,32},{32,40},{40,48},{48,56},{56,64},{64,7... | collective-permute-start | bytes 1769480 | tf_op jit(solution)/shard_map/ppermute | solution.py:10
  59.0 19.3 %collective-permute-start.1 = (bf16[6,192,256]{2,1,0:T(8,128)(2,1)}, bf16[6,192,256]{2,1,0:T(8,128)(2,1)}, u32[]{:S(2)}, u32[]{:S(2)}) collective-permute-start(bf16[6,192,256]{2,1,0:T(8,128)(2,1)} %gather_fusion.1), channel_id=1, source_target_pairs={{0,504},{8,0},{16,8},{24,16},{32,24},{40,32},{48,40},{56,48},{64,5... | collective-permute-start | bytes 1769480 | tf_op jit(solution)/shard_map/ppermute | solution.py:10
  86.6 3.1 copy-start.2
  89.6 0.9 copy-start.4
  90.5 109.9 %all-gather.8.cloned.1.call-start = ((), (), s32[]{:S(2)}) async-start(), calls=%async_computation.2 | async-start | bytes 2654208 | tf_op jit(solution)/shard_map/all_gather | solution.py:18
  128.1 21.5 %collective-permute-start.2 = (bf16[6,192,256]{2,1,0:T(8,128)(2,1)}, bf16[6,192,256]{2,1,0:T(8,128)(2,1)}, u32[]{:S(2)}, u32[]{:S(2)}) collective-permute-start(bf16[6,192,256]{2,1,0:T(8,128)(2,1)} %gather_fusion.3), channel_id=1, source_target_pairs={{0,8},{8,16},{16,24},{24,32},{32,40},{40,48},{48,56},{56,64},{64,7... | collective-permute-start | bytes 1769480 | tf_op jit(solution)/shard_map/ppermute | solution.py:10
  134.3 19.3 %collective-permute-start.3 = (bf16[6,192,256]{2,1,0:T(8,128)(2,1)}, bf16[6,192,256]{2,1,0:T(8,128)(2,1)S(1)}, u32[]{:S(2)}, u32[]{:S(2)}) collective-permute-start(bf16[6,192,256]{2,1,0:T(8,128)(2,1)} %gather_fusion.4), channel_id=1, source_target_pairs={{0,504},{8,0},{16,8},{24,16},{32,24},{40,32},{48,40},{56,48},{64,5... | collective-permute-start | bytes 1769480 | tf_op jit(solution)/shard_map/ppermute | solution.py:10
  161.8 3.1 copy-start.3
  161.8 3.1 copy-start.5
  166.0 152.0 %all-reduce.8.cloned.1.call-start = ((), (), s32[]{:S(2)}) async-start(), calls=%async_computation.4 | async-start | bytes 1048576 | tf_op jit(solution)/shard_map/psum | solution.py:49
  203.5 21.5 %collective-permute-start.4 = (bf16[6,192,256]{2,1,0:T(8,128)(2,1)}, bf16[6,192,256]{2,1,0:T(8,128)(2,1)}, u32[]{:S(2)}, u32[]{:S(2)}) collective-permute-start(bf16[6,192,256]{2,1,0:T(8,128)(2,1)} %gather_fusion.6), channel_id=1, source_target_pairs={{0,8},{8,16},{16,24},{24,32},{32,40},{40,48},{48,56},{56,64},{64,7... | collective-permute-start | bytes 1769480 | tf_op jit(solution)/shard_map/ppermute | solution.py:10
  209.7 19.3 %collective-permute-start.5 = (bf16[6,192,256]{2,1,0:T(8,128)(2,1)}, bf16[6,192,256]{2,1,0:T(8,128)(2,1)S(1)}, u32[]{:S(2)}, u32[]{:S(2)}) collective-permute-start(bf16[6,192,256]{2,1,0:T(8,128)(2,1)} %gather_fusion.7), channel_id=1, source_target_pairs={{0,504},{8,0},{16,8},{24,16},{32,24},{40,32},{48,40},{56,48},{64,5... | collective-permute-start | bytes 1769480 | tf_op jit(solution)/shard_map/ppermute | solution.py:10
  237.2 3.0 copy-start.1
  242.2 339.1 %all-reduce.6.cloned.1.call-start = ((), (), s32[]{:S(2)}) async-start(), calls=%async_computation.3 | async-start | bytes 1048576 | tf_op jit(solution)/shard_map/psum | solution.py:49
  586.0 0.7 copy-start.6
Sparse Core Ops, SparseCore 0:
  10.7 38.9 all-gather.3
  90.6 34.3 all-gather.5
  166.1 34.2 all-gather.7
  242.3 75.6 all-reduce.7
  321.3 259.8 all-reduce.5
